TPU v7x, 256 devices: a whole 4x4x8 slice. The times are simulated.
256 devices in a mesh: nodes: 64 (over x, z, core), feat: 4 (over y).
Axes of the slice: x: 4, y: 4, z: 8, core: 2. Of those that a mesh axis runs over, the one named last changes fastest.
Arguments:
- node_feats: bfloat16 [32768, 512], P('nodes', 'feat'), may hold values from -6 to 6
- weight_one: bfloat16 [512, 512], replicated, may hold values from -0.25 to 0.25
- weight_two: bfloat16 [512, 512], replicated, may hold values from -0.25 to 0.25
- adj_tiles: bfloat16 [256, 24, 128, 128], P('nodes'), may hold values from -0.109375 to 0.109375
- tile_owner: int32 [6144, 1], P('nodes'), may hold values from 0 to 63; in each aligned block of 96 rows (0 to 95, 96 to 191, ...) at most 2 rows name the same one
- tile_local: int32 [6144, 1], P('nodes'), may hold values from 0 to 3
- cotangent: bfloat16 [32768, 512], P('nodes', 'feat'), may hold values from -6 to 6
Outputs:
- layer_output: bfloat16 [32768, 512], P('nodes', 'feat')
- grad_one: float32 [512, 512], P('feat')
- grad_two: float32 [512, 512], P('feat')
Inputs may be any that keep to these rules, and one draw needn't show every extreme that they name: `tile_owner`: among the 96 tiles of one index of nodes, each owner index is named by at most 2 tiles, and exactly 2 for some owner.
All inputs are finite; a program needn't handle non-finite values.
Results may differ from a plain program's by a relative error of at most 0.0065.
Values may be sent and summed in bfloat16 or wider, within the bound.
No kernel may reach another device: no remote copies, remote signals or barrier semaphores. Data moves between devices by JAX's collectives and lax.ppermute only.
A program may use at most 128 MiB of HBM per device.

v0:
```python
import math
import jax
import jax.numpy as jnp
from jax import lax
from jax.sharding import PartitionSpec as P


def plan_slots(tile_owner, tile_local, node_count, capacity):
    owners = tile_owner[:, 0]
    local_ids = tile_local[:, 0]
    hits = (owners[:, None] == jnp.arange(node_count, dtype=jnp.int32)[None, :]).astype(jnp.int32)
    earlier = jnp.cumsum(hits, axis=0) - hits
    ranks = jnp.sum(earlier * hits, axis=1)
    slots = owners * capacity + ranks
    table = jnp.full((node_count * capacity,), -1, jnp.int32).at[slots].set(local_ids)
    source = (
        jnp.zeros((node_count * capacity,), jnp.int32)
        .at[slots]
        .set(jnp.arange(owners.shape[0], dtype=jnp.int32))
    )
    return (slots, table.reshape(node_count, capacity), source)


def body(node_feats, weight_one, weight_two, adj_tiles, tile_owner, tile_local, cotangent):
    node_count = lax.axis_size("nodes")
    blocks_dev = adj_tiles.shape[0]
    per_block = adj_tiles.shape[1]
    block_size = adj_tiles.shape[2]
    tile_total = blocks_dev * per_block
    capacity = max(2, (4 * tile_total + 3 * node_count - 1) // (3 * node_count))
    width = node_feats.shape[1]
    feat_index = lax.axis_index("feat")
    slots, requests, source = plan_slots(tile_owner, tile_local, node_count, capacity)
    asked = lax.all_to_all(requests, "nodes", split_axis=0, concat_axis=0, tiled=True)
    columns = tile_owner[:, 0] * blocks_dev + tile_local[:, 0]

    def spread(features):
        whole = lax.all_gather(features, "nodes", axis=0, tiled=True)
        picked = whole.reshape(-1, block_size, width)[columns]
        picked = picked.reshape(blocks_dev, per_block, block_size, width)
        summed = jnp.einsum("bkij,bkjf->bif", adj_tiles, picked, preferred_element_type=jnp.float32)
        return summed.reshape(-1, width).astype(jnp.bfloat16)

    def mixing(propagated, weights):
        weight_rows = lax.dynamic_slice_in_dim(weights, feat_index * width, width, 0)
        partial_z = jnp.dot(propagated, weight_rows, preferred_element_type=jnp.float32)
        result = lax.psum_scatter(partial_z, "feat", scatter_dimension=1, tiled=True)
        return result

    prop_one = spread(node_feats)
    z_one = mixing(prop_one, weight_one)
    hidden = (z_one * jax.nn.sigmoid(z_one)).astype(jnp.bfloat16)
    prop_two = spread(hidden)
    layer_output = mixing(prop_two, weight_two).astype(jnp.bfloat16)
    factor = 1.0 / math.sqrt(node_feats.shape[0] * node_count)
    contract_rows = (((0,), (0,)), ((), ()))
    cot_full = lax.all_gather(cotangent, "feat", axis=1, tiled=True)
    grad_two = (
        lax.dot_general(prop_two, cot_full, contract_rows, preferred_element_type=jnp.float32)
        * factor
    )
    weight_slice = lax.dynamic_slice_in_dim(weight_two, feat_index * width, width, 0)
    grad_prop = lax.dot_general(
        cot_full, weight_slice, (((1,), (1,)), ((), ())), preferred_element_type=jnp.float32
    ).astype(jnp.bfloat16)
    grad_blocks = grad_prop.reshape(blocks_dev, block_size, width)
    terms = jnp.einsum("bkji,bjf->bkif", adj_tiles, grad_blocks, preferred_element_type=jnp.float32)
    packed = terms.reshape(tile_total, block_size, width)[source].reshape(
        node_count, capacity, block_size, width
    )
    returned = lax.all_to_all(packed, "nodes", split_axis=0, concat_axis=0, tiled=True)
    slot_terms = returned.reshape(-1, block_size, width)
    selector = (
        asked.reshape(-1)[:, None] == jnp.arange(blocks_dev, dtype=jnp.int32)[None, :]
    ).astype(jnp.float32)
    grad_hidden = jnp.einsum(
        "sl,sif->lif", selector, slot_terms, precision=lax.Precision.HIGHEST
    ).reshape(-1, width)
    sigma = jax.nn.sigmoid(z_one)
    grad_z = (grad_hidden * sigma * (1.0 + z_one * (1.0 - sigma))).astype(jnp.bfloat16)
    grad_full = lax.all_gather(grad_z, "feat", axis=1, tiled=True)
    grad_one = (
        lax.dot_general(prop_one, grad_full, contract_rows, preferred_element_type=jnp.float32)
        * factor
    )
    grad_one, grad_two = lax.psum((grad_one, grad_two), "nodes")
    return (layer_output, grad_one, grad_two)


def solution(mesh):
    placed = (
        P("nodes", "feat"),
        P(),
        P(),
        P("nodes", None, None, None),
        P("nodes", None),
        P("nodes", None),
        P("nodes", "feat"),
    )
    return jax.shard_map(
        body,
        mesh=mesh,
        in_specs=placed,
        out_specs=(P("nodes", "feat"), P("feat", None), P("feat", None)),
        check_vma=False,
    )
```

profile of v0, /device:TPU:2, one launch (start us, length us, event | category | flops | bytes accessed | tf_op | source)
XLA Modules:
  0.0 596.0 jit_solution(3835139693002042372)
XLA Ops:
  12.3 12.0 %all-to-all-start = ((s32[64,1,2]{2,1,0:T(1,128)}), s32[64,1,2]{2,1,0:T(1,128)S(1)}, u32[]{:S(2)}, u32[]{:S(2)}) async-start(s32[64,1,2]{2,1,0:T(1,128)} %bitcast.18), calls=%async_computation.2 | async-start | bytes 65536 | tf_op jit(solution)/shard_map/all_to_all | solution.py:34
  24.3 14.3 %all_gather.14 = bf16[512,512]{1,0:T(8,128)(2,1)S(1)} all-gather(bf16[512,128]{1,0:T(8,128)(2,1)} %param.13), channel_id=1, replica_groups=mesh['nodes'=64,'feat'=4] {'feat'}, dimensions={1}, use_global_device_ids=true | all-gather | bytes 655360 | tf_op jit(solution)/shard_map/all_gather | solution.py:57
  41.6 3.5 fusion.5
  45.1 6.6 %copy.27 = f32[96,128,128]{2,1,0:T(8,128)} copy(f32[96,128,128]{1,2,0:T(8,128)} %bitcast.65) | data formatting | bytes 12582912 | tf_op jit(solution)/shard_map/reshape | solution.py:68
  51.8 7.1 %gather_fusion.2 = f32[128,128,128]{2,1,0:T(8,128)} fusion(f32[96,128,128]{2,1,0:T(8,128)} %copy.27, s32[1024]{0:T(1024)S(1)} %pad_clamp_fusion), kind=kCustom, calls=%fused_computation.2 | custom fusion | bytes 16777728 | tf_op jit(solution)/shard_map/gather | solution.py:68
  58.8 15.3 %copy.28 = f32[64,2,128,128]{3,1,2,0:T(2,128)} copy(f32[64,2,128,128]{3,2,1,0:T(8,128)} %bitcast.63) | data formatting | bytes 16777216 | tf_op jit(solution)/shard_map/reshape | solution.py:68
  74.1 10.7 %all-to-all-start.1 = ((f32[64,2,128,128]{3,1,2,0:T(2,128)}), f32[64,2,128,128]{3,1,2,0:T(2,128)}, u32[]{:S(2)}, u32[]{:S(2)}) async-start(f32[64,2,128,128]{3,1,2,0:T(2,128)} %copy.28), calls=%async_computation.3 | async-start | bytes 16777216 | tf_op jit(solution)/shard_map/all_to_all | solution.py:71
  84.9 22.9 %all-gather.3.cloned.1.call-done = bf16[32768,128]{1,0:T(8,128)(2,1)} async-done(((bf16[512,128]{1,0:T(8,128)(2,1)}), bf16[32768,128]{1,0:T(8,128)(2,1)}) %all-gather.3.cloned.1.call-update) | async-done | bytes 8388624 | tf_op jit(solution)/shard_map/all_gather | solution.py:38
  107.8 6.2 %gather_fusion = bf16[96,128,128]{2,1,0:T(8,128)(2,1)} fusion(bf16[256,128,128]{2,1,0:T(8,128)(2,1)} %bitcast.72, s32[1024]{0:T(1024)S(1)} %pad_clamp_fusion.1), kind=kCustom, calls=%fused_computation | custom fusion | bytes 6291840 | tf_op jit(solution)/shard_map/gather | solution.py:39
  114.0 2.9 fusion
  116.8 2.1 fusion.7
  120.6 151.2 %all-to-all-done.1 = f32[64,2,128,128]{3,1,2,0:T(2,128)} async-done(((f32[64,2,128,128]{3,1,2,0:T(2,128)}), f32[64,2,128,128]{3,1,2,0:T(2,128)}, u32[]{:S(2)}, u32[]{:S(2)}) %all-to-all-start.1) | async-done | bytes 8388640 | tf_op jit(solution)/shard_map/all_to_all | solution.py:71
  271.8 6.1 %copy.29 = f32[64,2,128,128]{3,1,0,2:T(2,128)S(1)} copy(f32[64,2,128,128]{3,1,2,0:T(2,128)} %all-to-all-done.1) | data formatting | bytes 16777216 | tf_op jit(solution)/shard_map/all_to_all | solution.py:71
  277.9 2.8 fusion.14
  280.8 1.8 fusion.4
  282.6 80.6 %all-gather.5.cloned.1.call-done = bf16[32768,128]{1,0:T(8,128)(2,1)} async-done(((bf16[512,128]{1,0:T(8,128)(2,1)}), bf16[32768,128]{1,0:T(8,128)(2,1)}) %all-gather.5.cloned.1.call-update) | async-done | bytes 8388624 | tf_op jit(solution)/shard_map/all_gather | solution.py:38
  363.3 6.2 %gather_fusion.1 = bf16[96,128,128]{2,1,0:T(8,128)(2,1)} fusion(bf16[256,128,128]{2,1,0:T(8,128)(2,1)} %bitcast.73, s32[1024]{0:T(1024)S(1)} %pad_clamp_fusion.1), kind=kCustom, calls=%fused_computation.1 | custom fusion | bytes 6291840 | tf_op jit(solution)/shard_map/gather | solution.py:39
  369.4 2.9 fusion.1
  372.3 2.2 fusion.10
  374.6 16.3 %all_gather.15 = bf16[512,512]{1,0:T(8,128)(2,1)S(1)} all-gather(bf16[512,128]{1,0:T(8,128)(2,1)S(1)} %copy-done.2), channel_id=1, replica_groups=mesh['nodes'=64,'feat'=4] {'feat'}, dimensions={1}, use_global_device_ids=true | all-gather | bytes 655360 | tf_op jit(solution)/shard_map/all_gather | solution.py:81
  391.8 2.0 convolution_multiply_fusion
  393.8 6.3 %reduce-scatter.5.cloned.1.call-done = f32[512,128]{1,0:T(8,128)} async-done(((f32[512,512]{1,0:T(8,128)}), f32[512,128]{1,0:T(8,128)}) %reduce-scatter.5.cloned.1.call-update) | async-done | bytes 262160 | tf_op jit(solution)/shard_map/reduce_scatter | solution.py:47
  401.8 184.4 %all-reduce.3.cloned.1.call-done = (f32[128,512]{1,0:T(8,128)}, f32[128,512]{1,0:T(8,128)}) async-done(((f32[128,512]{1,0:T(8,128)}, f32[128,512]{1,0:T(8,128)}), (f32[128,512]{1,0:T(8,128)}, f32[128,512]{1,0:T(8,128)})) %all-reduce.3.cloned.1.call-update) | async-done | bytes 524304 | tf_op jit(solution)/shard_map/psum | solution.py:86
  586.2 1.7 copy.40
  (38 shorter events, 14.1 us)
Async XLA Ops:
  7.2 34.4 %copy-start = (bf16[4,24,128,128]{3,2,1,0:T(8,128)(2,1)S(1)}, bf16[4,24,128,128]{3,2,1,0:T(8,128)(2,1)}, u32[]{:S(2)}) copy-start(bf16[4,24,128,128]{3,2,1,0:T(8,128)(2,1)} %param.10) | copy-start | bytes 9437188
  7.2 100.6 %all-gather.3.cloned.1.call-start = ((), (), s32[]{:S(2)}) async-start(), calls=%async_computation.4 | async-start | bytes 8519680 | tf_op jit(solution)/shard_map/all_gather | solution.py:38
  12.3 61.9 %all-to-all-start = ((s32[64,1,2]{2,1,0:T(1,128)}), s32[64,1,2]{2,1,0:T(1,128)S(1)}, u32[]{:S(2)}, u32[]{:S(2)}) async-start(s32[64,1,2]{2,1,0:T(1,128)} %bitcast.18), calls=%async_computation.2 | async-start | bytes 65536 | tf_op jit(solution)/shard_map/all_to_all | solution.py:34
  38.6 0.8 copy-start.1
  74.1 197.6 %all-to-all-start.1 = ((f32[64,2,128,128]{3,1,2,0:T(2,128)}), f32[64,2,128,128]{3,1,2,0:T(2,128)}, u32[]{:S(2)}, u32[]{:S(2)}) async-start(f32[64,2,128,128]{3,1,2,0:T(2,128)} %copy.28), calls=%async_computation.3 | async-start | bytes 16777216 | tf_op jit(solution)/shard_map/all_to_all | solution.py:71
  84.8 195.9 %reduce-scatter.3.cloned.1.call-start = ((), (), s32[]{:S(2)}) async-start(), calls=%async_computation.5 | async-start | bytes 1310720 | tf_op jit(solution)/shard_map/reduce_scatter | solution.py:47
  119.0 244.3 %all-gather.5.cloned.1.call-start = ((), (), s32[]{:S(2)}) async-start(), calls=%async_computation.6 | async-start | bytes 8519680 | tf_op jit(solution)/shard_map/all_gather | solution.py:38
  282.6 117.5 %reduce-scatter.5.cloned.1.call-start = ((), (), s32[]{:S(2)}) async-start(), calls=%async_computation.7 | async-start | bytes 1310720 | tf_op jit(solution)/shard_map/reduce_scatter | solution.py:47
  369.4 5.1 copy-start.2
  374.5 211.7 %all-reduce.3.cloned.1.call-start = ((), (), s32[]{:S(2)}) async-start(), calls=%async_computation.8 | async-start | bytes 1048576 | tf_op jit(solution)/shard_map/psum | solution.py:86
Sparse Core Ops, SparseCore 0:
  10.8 96.9 all-gather.2
  119.1 28.1 reduce-scatter.2
  282.7 80.4 all-gather.4
  374.6 25.4 reduce-scatter.4
  404.1 182.0 all-reduce.2
where the time goes:
time: 597 us; the launch traced here: 596 us
  waiting for transfers between devices  446 us (75%)
  local copies, waits for them, and re-layouts  54.9 us (9%)
  blocking collectives  30.6 us (5%)
  starting transfers between devices  23.1 us (4%)
  matrix products  20.6 us (3%)
  between operations  13.9 us (2%)
  other arithmetic  6.74 us (1%)
    psum x1, waiting for transfers between devices, body(): grad_one, grad_two = lax.psum((grad_one, grad_two), 'nodes')  184 us
    all_to_all x1, waiting for transfers between devices, body(): lax.all_to_all(packed, 'nodes', split_axis=0, concat_axis=0, tiled=True)  151 us
    all_gather x2, waiting for transfers between devices, spread(): whole = lax.all_gather(features, 'nodes', axis=0, tiled=True)  104 us
    reshape x2, local copies, waits for them, and re-layouts, body(): terms.reshape(tile_total, block_size, width)[source]  22 us
    all_gather x1, blocking collectives, body(): grad_full = lax.all_gather(grad_z, 'feat', axis=1, tiled=True)  16.3 us
    all_gather x1, blocking collectives, body(): cot_full = lax.all_gather(cotangent, 'feat', axis=1, tiled=True)  14.3 us
    gather x2, local copies, waits for them, and re-layouts, spread(): picked = whole.reshape(-1, block_size, width)[columns]  12.3 us
    all_to_all x1, starting transfers between devices, body(): lax.all_to_all(requests, 'nodes', split_axis=0, concat_axis=0, tiled=True)  12 us
  transfers between devices with their start and end apart: 7, of which 5 were waited for; matrix products, arithmetic and copies ran while one was open for 11% of the time, Pallas kernels for 0%

commit v1 on v0

--- a/solution.py
+++ b/solution.py
@@ -35,7 +35,10 @@
     columns = tile_owner[:, 0] * blocks_dev + tile_local[:, 0]
 
     def spread(features):
-        whole = lax.all_gather(features, "nodes", axis=0, tiled=True)
+        size = lax.axis_size("nodes")
+        pieces = jnp.stack([features for _ in range(size)])
+        pieces = lax.all_to_all(pieces, "nodes", split_axis=0, concat_axis=0)
+        whole = jnp.concatenate(pieces, axis=0)
         picked = whole.reshape(-1, block_size, width)[columns]
         picked = picked.reshape(blocks_dev, per_block, block_size, width)
         summed = jnp.einsum("bkij,bkjf->bif", adj_tiles, picked, preferred_element_type=jnp.float32)

time: 597 us -> 859 us (1.44)
  blocking collectives: 30.6 us -> 242 us
  waiting for transfers between devices: 446 us -> 497 us
  starting transfers between devices: 23.1 us -> 14.5 us
    all_to_all x0 -> x2, blocking collectives: none -> 212 us  [the longest x1 191 us: spread(): pieces = lax.all_to_all(pieces, 'nodes', split_axis=0, concat_axis=0)]
    all_to_all x1, waiting for transfers between devices: 0.01 us -> 135 us  [spread(): pieces = lax.all_to_all(pieces, 'nodes', split_axis=0, concat_axis=0)]
    all_gather x2 -> x0, waiting for transfers between devices: 104 us -> none  [spread(): whole = lax.all_gather(features, 'nodes', axis=0, tiled=True)]
    all_to_all x1, waiting for transfers between devices: 151 us -> 171 us  [body(): lax.all_to_all(packed, 'nodes', split_axis=0, concat_axis=0, tiled=True)]
  transfers between devices with their start and end apart: 7 -> 5, of which waited for: 5 -> 4; matrix products, arithmetic and copies ran while one was open for 11% -> 7% of each run, Pallas kernels for 0% -> 0%
where the time goes in v1:
time: 859 us; the launch traced here: 858 us
  waiting for transfers between devices  497 us (58%)
  blocking collectives  242 us (28%)
  local copies, waits for them, and re-layouts  62.5 us (7%)
  matrix products  20.7 us (2%)
  starting transfers between devices  14.5 us (2%)
  between operations  13.9 us (2%)
    all_to_all x1, blocking collectives, spread(): pieces = lax.all_to_all(pieces, 'nodes', split_axis=0, concat_axis=0)  191 us
    psum x1, waiting for transfers between devices, body(): grad_one, grad_two = lax.psum((grad_one, grad_two), 'nodes')  184 us
    all_to_all x1, waiting for transfers between devices, body(): lax.all_to_all(packed, 'nodes', split_axis=0, concat_axis=0, tiled=True)  171 us
    all_to_all x1, waiting for transfers between devices, spread(): pieces = lax.all_to_all(pieces, 'nodes', split_axis=0, concat_axis=0)  135 us
    reshape x2, local copies, waits for them, and re-layouts, body(): terms.reshape(tile_total, block_size, width)[source]  21.9 us
    all_to_all x1, blocking collectives, body(): lax.all_to_all(requests, 'nodes', split_axis=0, concat_axis=0, tiled=True)  20.4 us
  transfers between devices with their start and end apart: 5, of which 4 were waited for; matrix products, arithmetic and copies ran while one was open for 7% of the time, Pallas kernels for 0%

profile of v1, /device:TPU:2, one launch (start us, length us, event | category | flops | bytes accessed | tf_op | source)
XLA Modules:
  0.0 857.7 jit_solution(5115311893587993138)
XLA Ops:
  10.9 20.4 %all_to_all.24 = s32[64,1,2]{2,1,0:T(1,128)S(1)} all-to-all(s32[64,1,2]{2,1,0:T(1,128)S(1)} %bitcast.76), channel_id=1, replica_groups=mesh['nodes'=64,'feat'=4] {'nodes'}, dimensions={0} | all-to-all | bytes 1024 | tf_op jit(solution)/shard_map/all_to_all | solution.py:34
  31.3 6.1 stack.4
  37.5 6.7 all-to-all-start
  45.1 14.0 %all_gather.6 = bf16[512,512]{1,0:T(8,128)(2,1)S(1)} all-gather(bf16[512,128]{1,0:T(8,128)(2,1)S(1)} %copy-done.3), channel_id=1, replica_groups=mesh['nodes'=64,'feat'=4] {'feat'}, dimensions={1}, use_global_device_ids=true | all-gather | bytes 655360 | tf_op jit(solution)/shard_map/all_gather | solution.py:60
  61.2 3.6 fusion.5
  64.8 6.6 copy.27
  71.4 7.1 gather_fusion.2
  78.5 15.3 %copy.28 = f32[64,2,128,128]{3,1,2,0:T(2,128)} copy(f32[64,2,128,128]{3,2,1,0:T(8,128)} %bitcast.65) | data formatting | bytes 16777216 | tf_op jit(solution)/shard_map/reshape | solution.py:71
  93.8 134.6 %all-to-all-done = bf16[64,512,128]{2,1,0:T(8,128)(2,1)} async-done(((bf16[64,512,128]{2,1,0:T(8,128)(2,1)}), bf16[64,512,128]{2,1,0:T(8,128)(2,1)}, u32[]{:S(2)}, u32[]{:S(2)}) %all-to-all-start) | async-done | bytes 8388640 | tf_op jit(solution)/shard_map/all_to_all | solution.py:40
  228.4 7.5 all-to-all-start.3
  236.0 6.2 gather_fusion
  242.2 2.9 fusion
  245.0 2.2 fusion.7
  248.8 171.3 %all-to-all-done.3 = f32[64,2,128,128]{3,1,2,0:T(2,128)} async-done(((f32[64,2,128,128]{3,1,2,0:T(2,128)}), f32[64,2,128,128]{3,1,2,0:T(2,128)}, u32[]{:S(2)}, u32[]{:S(2)}) %all-to-all-start.3) | async-done | bytes 8388640 | tf_op jit(solution)/shard_map/all_to_all | solution.py:74
  420.2 6.1 copy.29
  426.3 2.8 fusion.14
  430.9 2.0 stack.5
  432.9 191.3 %all_to_all.25 = bf16[64,512,128]{2,1,0:T(8,128)(2,1)} all-to-all(bf16[64,512,128]{2,1,0:T(8,128)(2,1)S(1)} %stack.5), channel_id=1, replica_groups=mesh['nodes'=64,'feat'=4] {'nodes'}, dimensions={0} | all-to-all | bytes 16777216 | tf_op jit(solution)/shard_map/all_to_all | solution.py:40
  624.2 6.2 gather_fusion.1
  630.4 2.9 fusion.1
  633.3 2.2 fusion.10
  635.6 16.4 %all_gather.7 = bf16[512,512]{1,0:T(8,128)(2,1)S(1)} all-gather(bf16[512,128]{1,0:T(8,128)(2,1)S(1)} %copy-done.2), channel_id=1, replica_groups=mesh['nodes'=64,'feat'=4] {'feat'}, dimensions={1}, use_global_device_ids=true | all-gather | bytes 655360 | tf_op jit(solution)/shard_map/all_gather | solution.py:84
  655.0 7.1 reduce-scatter.5.cloned.1.call-done
  663.7 184.2 %all-reduce.3.cloned.1.call-done = (f32[128,512]{1,0:T(8,128)}, f32[128,512]{1,0:T(8,128)}) async-done(((f32[128,512]{1,0:T(8,128)}, f32[128,512]{1,0:T(8,128)}), (f32[128,512]{1,0:T(8,128)}, f32[128,512]{1,0:T(8,128)})) %all-reduce.3.cloned.1.call-update) | async-done | bytes 524304 | tf_op jit(solution)/shard_map/psum | solution.py:89
  (38 shorter events, 18.1 us)
Async XLA Ops:
  7.2 54.0 %copy-start = (bf16[4,24,128,128]{3,2,1,0:T(8,128)(2,1)S(1)}, bf16[4,24,128,128]{3,2,1,0:T(8,128)(2,1)}, u32[]{:S(2)}) copy-start(bf16[4,24,128,128]{3,2,1,0:T(8,128)(2,1)} %param.10) | copy-start | bytes 9437188
  37.5 7.6 copy-start.3
  37.5 191.0 %all-to-all-start = ((bf16[64,512,128]{2,1,0:T(8,128)(2,1)}), bf16[64,512,128]{2,1,0:T(8,128)(2,1)}, u32[]{:S(2)}, u32[]{:S(2)}) async-start(bf16[64,512,128]{2,1,0:T(8,128)(2,1)} %stack.4), calls=%async_computation | async-start | bytes 16777216 | tf_op jit(solution)/shard_map/all_to_all | solution.py:40
  59.1 0.8 copy-start.1
  228.4 191.7 %all-to-all-start.3 = ((f32[64,2,128,128]{3,1,2,0:T(2,128)}), f32[64,2,128,128]{3,1,2,0:T(2,128)}, u32[]{:S(2)}, u32[]{:S(2)}) async-start(f32[64,2,128,128]{3,1,2,0:T(2,128)} %copy.28), calls=%async_computation.5 | async-start | bytes 16777216 | tf_op jit(solution)/shard_map/all_to_all | solution.py:74
  235.9 193.2 %reduce-scatter.3.cloned.1.call-start = ((), (), s32[]{:S(2)}) async-start(), calls=%async_computation.6 | async-start | bytes 1310720 | tf_op jit(solution)/shard_map/reduce_scatter | solution.py:50
  247.2 414.8 %reduce-scatter.5.cloned.1.call-start = ((), (), s32[]{:S(2)}) async-start(), calls=%async_computation.7 | async-start | bytes 1310720 | tf_op jit(solution)/shard_map/reduce_scatter | solution.py:50
  630.4 5.2 copy-start.2
  635.5 212.3 %all-reduce.3.cloned.1.call-start = ((), (), s32[]{:S(2)}) async-start(), calls=%async_computation.8 | async-start | bytes 1048576 | tf_op jit(solution)/shard_map/psum | solution.py:89
Sparse Core Ops, SparseCore 0:
  247.3 27.5 reduce-scatter.2
  635.6 26.3 reduce-scatter.4
  666.2 181.5 all-reduce.2
